TPU v7x, 32 devices: a whole 2x2x4 slice. The times are simulated.
32 devices in a mesh: layer: 2 (over x), band: 16 (over z, y, core).
Axes of the slice: x: 2, y: 2, z: 4, core: 2. Of those that a mesh axis runs over, the one named last changes fastest.
Arguments:
- coeffs: bfloat16 [32, 128, 10240], P('layer', None, 'band'), may hold values from -6 to 6
- hamilton: bfloat16 [32, 7, 128, 128], P('layer'), may hold values from -0.1875 to 0.1875
- neighbors: int32 [32, 7], P('layer'), may hold values from -1 to 31, as said below
- basis: bfloat16 [32, 1728, 128], P(('layer', 'band')), may hold values from -0.5 to 0.5
- occupation: int32 [10240], replicated, may hold values from 0 to 3
Outputs:
- filtered: bfloat16 [32, 128, 10240], P('layer', None, 'band')
- density: float32 [32, 1728], P(('layer', 'band'))
Inputs may be any that keep to these rules, and one draw needn't show every extreme that they name: `neighbors`: column 0 of row e is e itself; columns 1 to 4 are its neighbours along the two periodic in-plane directions, all in e's plane of 16 elements (rows e // 16 * 16 to that plus 16 - 1); columns 5 and 6 are the elements at the same lattice site in the previous and the next plane, -1 before the first and after the last plane. The numbering of sites within each plane is drawn.
All inputs are finite; a program needn't handle non-finite values.
Results may differ from a plain program's by a relative error of at most 0.0042.
Values may be sent and summed in bfloat16 or wider, within the bound.
A program may use at most 64 MiB of HBM per device.

v0:
```python
import functools

import jax
import jax.numpy as jnp
from jax import lax
from jax.experimental import pallas as pl
from jax.experimental.pallas import tpu as pltpu
from jax.sharding import PartitionSpec as P

FY = 4
FZ = 4
MESH = pl.DeviceIdType.MESH

center = 0.5
half_width = 1.5


def with_halo(array, sides, width):
    for axis, dim in sides:
        devices, length = (lax.axis_size(axis), array.shape[dim])
        up = [(i, (i + 1) % devices) for i in range(devices - 1)]
        down = [(j, i) for i, j in up]
        last = lax.slice_in_dim(array, length - width, length, axis=dim)
        first = lax.slice_in_dim(array, 0, width, axis=dim)
        before = lax.ppermute(last, axis, up)
        after = lax.ppermute(first, axis, down)
        array = jnp.concatenate([before, array, after], axis=dim)
    return array


def neighbor_product(blocks, nearby):
    return jnp.einsum("ekij,ekjb->eib", blocks, nearby, preferred_element_type=jnp.float32)


def general_body(coeffs, hamilton, neighbors, basis, occupation):
    elements = coeffs.shape[0]
    face_size = FY * FZ
    offset = lax.axis_index("layer") * elements - face_size
    usable = neighbors >= 0
    position = jnp.where(usable, neighbors - offset, 0)
    allowed = usable.astype(jnp.bfloat16)

    def operate(source):
        padded = with_halo(source, (("layer", 0),), face_size)
        inside = source[position[:, :5] - face_size]
        result = neighbor_product(hamilton[:, :5], inside)
        across = padded[position[:, 5:]] * allowed[:, 5:, None, None]
        return result + neighbor_product(hamilton[:, 5:], across)

    start_vals = coeffs.astype(jnp.float32)
    first_image = operate(coeffs)
    filtered_once = ((first_image - center * start_vals) / half_width).astype(jnp.bfloat16)
    second_image = operate(filtered_once)
    filtered = (
        2.0 * (second_image - center * filtered_once.astype(jnp.float32)) / half_width - start_vals
    ).astype(jnp.bfloat16)
    weights = (1 + occupation).astype(jnp.float32) / (2.0 * occupation.shape[0])
    copies = lax.axis_size("band") // elements
    duplicated = jnp.tile(filtered, (copies, 1, 1))
    regrouped = lax.all_to_all(duplicated, "band", split_axis=0, concat_axis=2, tiled=True)
    orbital = jnp.dot(basis[0], regrouped[0], preferred_element_type=jnp.float32)
    density = jnp.sum(orbital * orbital * weights[None, :], axis=1)[None, :]
    return (filtered, density)


def kernel(spans, nb, c_hbm, h_hbm, nbr_hbm, occ_ref, filt_hbm, total_ref, *scratch):
    count = len(spans)
    cown, cx, f1o, f1x, outv = (scratch[i * count:(i + 1) * count] for i in range(5))
    (hown, hx, nx_v, nown, nx, gram, gsend, gcore, grecv,
     c_send, c_recv, hx_send, hx_recv, n_send, n_recv, f_send, f_recv, k_send, k_recv, g_send, g_recv,
     lc_sem, lh_sem, lo_sem, misc_sem) = scratch[5 * count:]
    elements = c_hbm.shape[0]
    nbl = c_hbm.shape[2]
    layer, b = lax.axis_index("layer"), lax.axis_index("band")
    other = 1 - layer
    nz = nb // 4
    z, y, core = b // 4, (b // 2) % 2, b % 2
    own_cross, x_cross = 6 - layer, 6 - other

    def ident(zz, yy, cc):
        return zz * 4 + yy * 2 + cc

    n_copy = pltpu.make_async_copy(nbr_hbm, nown, misc_sem.at[0])
    n_copy.start()
    c_copies = []
    h_copies = [
        pltpu.make_async_copy(h_hbm.at[:, pl.ds(0, 5)], hown.at[:, pl.ds(0, 5)], lh_sem.at[0]),
        pltpu.make_async_copy(h_hbm.at[:, pl.ds(own_cross, 1)], hown.at[:, pl.ds(5, 1)], lh_sem.at[1]),
    ]

    barrier = pltpu.get_barrier_semaphore()
    pl.semaphore_signal(barrier, inc=1, device_id={"layer": other, "band": b}, device_id_type=MESH)
    half = nb // 2
    site = b // 2
    core_peer = b + 1 - 2 * core
    for peer in [core_peer] + [(site + k) % half * 2 + core for k in range(1, half)]:
        pl.semaphore_signal(barrier, inc=1, device_id={"layer": layer, "band": peer}, device_id_type=MESH)
    pl.semaphore_wait(barrier, half + 1)

    def to_x(src, dst, send, recv):
        return pltpu.make_async_remote_copy(
            src_ref=src, dst_ref=dst, send_sem=send, recv_sem=recv,
            device_id={"layer": other, "band": b}, device_id_type=MESH)

    def to_band(src, dst, send, recv, peer):
        return pltpu.make_async_remote_copy(
            src_ref=src, dst_ref=dst, send_sem=send, recv_sem=recv,
            device_id={"layer": layer, "band": peer}, device_id_type=MESH)

    h_across = [
        to_x(h_hbm.at[b, pl.ds(0, 5)], hx.at[b, pl.ds(0, 5)], hx_send.at[0], hx_recv.at[0]),
        to_x(h_hbm.at[b, pl.ds(own_cross, 1)], hx.at[b, pl.ds(5, 1)], hx_send.at[1], hx_recv.at[1]),
    ]
    n_across = to_x(nbr_hbm, nx_v, n_send.at[0], n_recv.at[0])
    c_across = [
        to_x(c_hbm.at[:, :, pl.ds(lo, n)], cx[i], c_send.at[i], c_recv.at[i])
        for i, (lo, n) in enumerate(spans)
    ]
    for copy in h_across + [n_across] + c_across:
        copy.start()
    for i, (lo, n) in enumerate(spans):
        copy = pltpu.make_async_copy(c_hbm.at[:, :, pl.ds(lo, n)], cown[i], lc_sem.at[i])
        copy.start()
        c_copies.append(copy)
    for copy in h_copies:
        copy.start()

    sent = []

    def forward(block, peer):
        slot = len(sent)
        copy = to_band(hx.at[block], hx.at[block], f_send.at[slot], f_recv.at[block], peer)
        copy.start()
        sent.append(copy)

    def arrived(block, peer):
        to_band(hx.at[block], hx.at[block], f_send.at[0], f_recv.at[block], peer).wait_recv()

    y_peer = ident(z, 1 - y, core)
    for copy in h_across:
        copy.wait_recv()
    for k in range(1, nz):
        forward(b, ident((z + k) % nz, y, core))
    forward(b, y_peer)
    forward(b, core_peer)
    for k in range(1, nz):
        block = ident((z - k + nz) % nz, y, core)
        arrived(block, block)
        forward(block, y_peer)
        forward(block, core_peer)
    for k in range(nz):
        block = ident((z - k + nz) % nz, 1 - y, core)
        arrived(block, y_peer)
        forward(block, core_peer)
    for k in range(nz):
        for yy in (y, 1 - y):
            arrived(ident((z - k + nz) % nz, yy, 1 - core), core_peer)

    n_across.wait_recv()
    nx_copy = pltpu.make_async_copy(nx_v, nx, misc_sem.at[1])
    nx_copy.start()
    n_copy.wait()
    nx_copy.wait()
    for copy in h_copies:
        copy.wait()

    def image(blocks, table, e, cross, near, far):
        row = jnp.concatenate([blocks[e, k] for k in range(6)], axis=1)
        parts = [near[lax.rem(table[k, e], elements)] for k in range(5)]
        parts.append(far[lax.rem(table[cross, e], elements)])
        return jnp.dot(row, jnp.concatenate(parts, axis=0), preferred_element_type=jnp.float32)

    out_copies = []
    for i, (lo, n) in enumerate(spans):
        c_copies[i].wait()
        c_across[i].wait_recv()

        last = i == count - 1
        start = pl.multiple_of(b * nbl + lo, 128)
        weight = (1 + occ_ref[:, pl.ds(start, n)]).astype(jnp.float32)

        def first_own(e):
            got = image(hown, nown, e, own_cross, cown[i], cx[i])
            return ((got - center * cown[i][e].astype(jnp.float32)) * (1.0 / half_width)).astype(jnp.bfloat16)

        def first_x(e):
            got = image(hx, nx, e, x_cross, cx[i], cown[i])
            return ((got - center * cx[i][e].astype(jnp.float32)) * (1.0 / half_width)).astype(jnp.bfloat16)

        step = 2 if last and elements % 2 == 0 else 1

        def first(t, carry):
            at = [t * step + u for u in range(step)]
            mine = [first_own(e) for e in at]
            theirs = [first_x(e) for e in at]
            for e, a, c in zip(at, mine, theirs):
                f1o[i][e] = a
                f1x[i][e] = c
            return carry

        def second(e):
            got = image(hown, nown, e, own_cross, f1o[i], f1x[i])
            once = f1o[i][e].astype(jnp.float32)
            value = (got - center * once) * (2.0 / half_width) - cown[i][e].astype(jnp.float32)
            value = value.astype(jnp.bfloat16)
            scaled = (value.astype(jnp.float32) * weight).astype(jnp.bfloat16)
            part = lax.dot_general(scaled, value, (((1,), (1,)), ((), ())), preferred_element_type=jnp.float32)
            return value, part + gram[e] if i > 0 else part

        def second_plain(s, carry):
            at = [2 * s, 2 * s + 1]
            got = [second(e) for e in at]
            for e, (value, part) in zip(at, got):
                outv[i][e] = value
                gram[e] = part
            return carry

        def to_core(t):
            return to_band(gsend.at[2 * t + 1 - core], gcore.at[t], k_send.at[t], k_recv.at[t], core_peer)

        def to_owner(k):
            element = (site + k) % half * 2 + core
            return to_band(gsend.at[element], grecv.at[k], g_send.at[k], g_recv.at[k], element)

        def pair_up(s, carry):
            at = [2 * s, 2 * s + 1]
            got = [second(2 * t + 1 - core) for t in at]
            for t, (value, part) in zip(at, got):
                outv[i][2 * t + 1 - core] = value
                gsend[2 * t + 1 - core] = part.astype(jnp.bfloat16)
                to_core(t).start()
            return carry

        def hand_over(ks):
            places = [(site + k) % half for k in ks]
            got = [second(2 * t + core) for t in places]
            for k, t, (value, part) in zip(ks, places, got):
                outv[i][2 * t + core] = value
                to_core(t).wait_recv()
                part = part + gcore[t].astype(jnp.float32)
                if isinstance(k, int) and k == half:
                    gram[2 * t + core] = part
                else:
                    gsend[2 * t + core] = part.astype(jnp.bfloat16)
                    to_owner(k).start()

        def hand_over_two(s, carry):
            hand_over([2 * s + 1, 2 * s + 2])
            return carry

        lax.fori_loop(0, elements // step, first, 0)
        if last:
            lax.fori_loop(0, half // 2, pair_up, 0)
            lax.fori_loop(0, half // 2 - 1, hand_over_two, 0)
            hand_over([half - 1, half])
        else:
            lax.fori_loop(0, elements // 2, second_plain, 0)
        copy = pltpu.make_async_copy(outv[i], filt_hbm.at[:, :, pl.ds(lo, n)], lo_sem.at[i])
        copy.start()
        out_copies.append(copy)

    total = gram[b]
    for k in range(1, half):
        to_owner(k).wait_recv()
        total = total + grecv[k].astype(jnp.float32)
    total_ref[...] = total * (1.0 / (2.0 * nbl * nb))

    for copy in h_across + [n_across] + c_across + sent:
        copy.wait_send()
    for t in range(half):
        to_core(t).wait_send()
    for k in range(1, half):
        to_owner(k).wait_send()
    for copy in out_copies:
        copy.wait()


def finish_kernel(pieces, filt_hbm, total_ref, basis_ref, out_hbm, dens_ref, held, in_sem, out_sem):
    size = held.shape[0] // pieces
    spans = [pl.ds(i * size, size) for i in range(pieces)]
    loads = [pltpu.make_async_copy(filt_hbm.at[at], held.at[at], in_sem.at[i]) for i, at in enumerate(spans)]
    stores = [pltpu.make_async_copy(held.at[at], out_hbm.at[at], out_sem.at[i]) for i, at in enumerate(spans)]
    for load in loads:
        load.start()
    for load, store in zip(loads, stores):
        load.wait()
        store.start()
    total = total_ref[...]
    high = total.astype(jnp.bfloat16)
    low = (total - high.astype(jnp.float32)).astype(jnp.bfloat16)
    functions = basis_ref[0]
    image_g = jnp.dot(functions, high, preferred_element_type=jnp.float32)
    image_g = image_g + jnp.dot(functions, low, preferred_element_type=jnp.float32)
    product = image_g * functions.astype(jnp.float32)
    top = product.astype(jnp.bfloat16)
    rest = (product - top.astype(jnp.float32)).astype(jnp.bfloat16)
    ones = jnp.ones((16, product.shape[1]), jnp.bfloat16)
    over_last = (((1,), (1,)), ((), ()))
    density = lax.dot_general(ones, top, over_last, preferred_element_type=jnp.float32)
    density = density + lax.dot_general(ones, rest, over_last, preferred_element_type=jnp.float32)
    dens_ref[...] = density[0:1]
    for store in stores:
        store.wait()


def plane_body(nb, coeffs, hamilton, neighbors, basis, occupation):
    elements, nbasis, nbl = coeffs.shape
    points = basis.shape[1]
    spans, lo = [], 0
    while lo < nbl:
        n = min(256, nbl - lo)
        spans.append((lo, n))
        lo += n
    count = len(spans)
    width = neighbors.shape[1]
    pieces = 4 if elements % 4 == 0 else 1
    values = [pltpu.VMEM((elements, nbasis, n), jnp.bfloat16) for _, n in spans]
    dma = pltpu.SemaphoreType.DMA
    hbm = pl.BlockSpec(memory_space=pl.ANY)
    vmem = pl.BlockSpec(memory_space=pltpu.VMEM)
    forwards = (nb // 4 - 1) + 2 + 2 * (nb // 4 - 1) + nb // 4
    spread, total = pl.pallas_call(
        functools.partial(kernel, spans, nb),
        out_shape=(
            jax.ShapeDtypeStruct(coeffs.shape, jnp.bfloat16),
            jax.ShapeDtypeStruct((nbasis, nbasis), jnp.float32),
        ),
        in_specs=[hbm, hbm, hbm, vmem],
        out_specs=(hbm, vmem),
        scratch_shapes=values * 5 + [
            pltpu.VMEM((elements, 6, nbasis, nbasis), jnp.bfloat16),
            pltpu.VMEM((elements, 6, nbasis, nbasis), jnp.bfloat16),
            pltpu.VMEM((width, elements), jnp.int32),
            pltpu.SMEM((width, elements), jnp.int32),
            pltpu.SMEM((width, elements), jnp.int32),
            pltpu.VMEM((elements, nbasis, nbasis), jnp.float32),
            pltpu.VMEM((elements, nbasis, nbasis), jnp.bfloat16),
            pltpu.VMEM((nb // 2, nbasis, nbasis), jnp.bfloat16),
            pltpu.VMEM((nb // 2, nbasis, nbasis), jnp.bfloat16),
            dma((count,)), dma((count,)),
            dma((2,)), dma((2,)),
            dma((1,)), dma((1,)),
            dma((forwards,)), dma((nb,)),
            dma((nb // 2,)), dma((nb // 2,)),
            dma((nb // 2,)), dma((nb // 2,)),
            dma((count,)), dma((2,)), dma((count,)), dma((2,)),
        ],
        compiler_params=pltpu.CompilerParams(collective_id=0, has_side_effects=True),
    )(coeffs, hamilton, neighbors.T, occupation.reshape(1, -1))
    return pl.pallas_call(
        functools.partial(finish_kernel, pieces),
        out_shape=(
            jax.ShapeDtypeStruct(coeffs.shape, jnp.bfloat16),
            jax.ShapeDtypeStruct((1, points), jnp.float32),
        ),
        in_specs=[hbm, vmem, vmem],
        out_specs=(hbm, vmem),
        scratch_shapes=[pltpu.VMEM(coeffs.shape, jnp.bfloat16), dma((pieces,)), dma((pieces,))],
    )(spread, total, basis)


def solution(mesh):
    layers, nb = mesh.shape["layer"], mesh.shape["band"]

    def body(coeffs, hamilton, neighbors, basis, occupation):
        elements = coeffs.shape[0]
        one_kernel = (
            layers == 2 and elements == FY * FZ and nb == elements
            and nb % 4 == 0 and nb >= 8 and coeffs.shape[2] % 128 == 0 and basis.shape[0] == 1
        )
        if one_kernel:
            return plane_body(nb, coeffs, hamilton, neighbors, basis, occupation)
        return general_body(coeffs, hamilton, neighbors, basis, occupation)

    return jax.shard_map(
        body,
        mesh=mesh,
        in_specs=(
            P("layer", None, "band"),
            P("layer", None, None, None),
            P("layer", None),
            P(("layer", "band"), None, None),
            P(),
        ),
        out_specs=(P("layer", None, "band"), P(("layer", "band"), None)),
        check_vma=False,
    )
```

profile of v0, /device:TPU:0, one launch (start us, length us, event | category | flops | bytes accessed | tf_op | source)
XLA Modules:
  0.0 87.3 jit_solution(14075954367161675911)
XLA Ops:
  0.6 82.3 %shard_map.68 = (bf16[16,128,640]{2,1,0:T(8,128)(2,1)}, f32[128,128]{1,0:T(8,128)}) custom-call(bf16[16,128,640]{2,1,0:T(8,128)(2,1)} %c_hbm.1, bf16[16,7,128,128]{3,2,1,0:T(8,128)(2,1)} %h_hbm.1, s32[7,16]{1,0:T(8,128)} %bitcast.3, s32[1,10240]{1,0:T(1,128)} %bitcast.2), custom_call_target="tpu_custom_call" | custom-call | tf_op jit(solution)/shard_map/pallas_call | solution.py:322
  82.9 4.4 %shard_map.69 = (bf16[16,128,640]{2,1,0:T(8,128)(2,1)}, f32[1,1728]{1,0:T(1,128)}) custom-call(bf16[16,128,640]{2,1,0:T(8,128)(2,1)} %get-tuple-element.4.filt_hbm, f32[128,128]{1,0:T(8,128)} %get-tuple-element.5.total_ref, bf16[1,1728,128]{2,1,0:T(8,128)(2,1)} %basis_ref.1), custom_call_target="tpu_custom_call" | custom-call | tf_op jit(solution)/shard_map/pallas_call | solution.py:350
where the time goes:
time: 87.6 us; the launch traced here: 87.3 us
  Pallas kernels  86.7 us (99%)
    pallas_call x1, Pallas kernels, plane_body(): pl.pallas_call(functools.partial(kernel, spans, nb), out_shape=(jax.Shape...  82.3 us
    pallas_call x1, Pallas kernels, plane_body(): pl.pallas_call(functools.partial(finish_kernel, pieces), out_shape=(jax.S...  4.42 us

commit v1 on v0

v1 whole, which is shorter than its diff:
```python
import functools

import jax
import jax.numpy as jnp
from jax import lax
from jax.experimental import pallas as pl
from jax.experimental.pallas import tpu as pltpu
from jax.sharding import PartitionSpec as P

FY = 4
FZ = 4
MESH = pl.DeviceIdType.MESH

center = 0.5
half_width = 1.5


def with_halo(array, sides, width):
    for axis, dim in sides:
        devices, length = (lax.axis_size(axis), array.shape[dim])
        up = [(i, (i + 1) % devices) for i in range(devices - 1)]
        down = [(j, i) for i, j in up]
        last = lax.slice_in_dim(array, length - width, length, axis=dim)
        first = lax.slice_in_dim(array, 0, width, axis=dim)
        before = lax.ppermute(last, axis, up)
        after = lax.ppermute(first, axis, down)
        array = jnp.concatenate([before, array, after], axis=dim)
    return array


def neighbor_product(blocks, nearby):
    return jnp.einsum("ekij,ekjb->eib", blocks, nearby, preferred_element_type=jnp.float32)


def general_body(coeffs, hamilton, neighbors, basis, occupation):
    elements = coeffs.shape[0]
    face_size = FY * FZ
    offset = lax.axis_index("layer") * elements - face_size
    usable = neighbors >= 0
    position = jnp.where(usable, neighbors - offset, 0)
    allowed = usable.astype(jnp.bfloat16)

    def operate(source):
        padded = with_halo(source, (("layer", 0),), face_size)
        inside = source[position[:, :5] - face_size]
        result = neighbor_product(hamilton[:, :5], inside)
        across = padded[position[:, 5:]] * allowed[:, 5:, None, None]
        return result + neighbor_product(hamilton[:, 5:], across)

    start_vals = coeffs.astype(jnp.float32)
    first_image = operate(coeffs)
    filtered_once = ((first_image - center * start_vals) / half_width).astype(jnp.bfloat16)
    second_image = operate(filtered_once)
    filtered = (
        2.0 * (second_image - center * filtered_once.astype(jnp.float32)) / half_width - start_vals
    ).astype(jnp.bfloat16)
    weights = (1 + occupation).astype(jnp.float32) / (2.0 * occupation.shape[0])
    copies = lax.axis_size("band") // elements
    duplicated = jnp.tile(filtered, (copies, 1, 1))
    regrouped = lax.all_to_all(duplicated, "band", split_axis=0, concat_axis=2, tiled=True)
    orbital = jnp.dot(basis[0], regrouped[0], preferred_element_type=jnp.float32)
    density = jnp.sum(orbital * orbital * weights[None, :], axis=1)[None, :]
    return (filtered, density)


def kernel(nb, n, c_hbm, h_hbm, nbr_hbm, occ_hbm, basis_hbm, out_ref, dens_ref, *scratch):
    elements, _, nbl = c_hbm.shape
    count = nbl // n
    cown, cx = scratch[:count], scratch[count:2 * count]
    (f1o, f1x, hown, hx, nx_v, nown, nx, occ_v, functions, gram, across,
     gsend_a, gcore_a, grecv_a, gsend_b, gcore_b, grecv_b, total_out, total_in,
     c_send, c_recv, hx_send, hx_recv, n_send, n_recv, f_send, f_recv,
     ka_send, ka_recv, ga_send, ga_recv, kb_send, kb_recv, gb_send, gb_recv, t_send, t_recv,
     lc_sem, lh_sem, misc_sem, x_ready, all_in) = scratch[2 * count:]
    layer, b = lax.axis_index("layer"), lax.axis_index("band")
    other = 1 - layer
    nz = nb // 4
    half = nb // 2
    site = b // 2
    z, y, core = b // 4, (b // 2) % 2, b % 2
    core_peer = b + 1 - 2 * core
    own_cross, x_cross = 6 - layer, 6 - other
    last = count - 1

    def ident(zz, yy, cc):
        return zz * 4 + yy * 2 + cc

    def place(s, side=layer):
        return pl.multiple_of((s + side * (last - 2 * s)) * n, n)

    barrier = pltpu.get_barrier_semaphore()

    @pl.when(layer == 0)
    def _():
        pl.semaphore_signal(barrier, inc=1, device_id={"layer": other, "band": b}, device_id_type=MESH)

    @pl.when(layer == 1)
    def _():
        pl.semaphore_wait(barrier, 1)
        pl.semaphore_signal(x_ready, inc=1, device_id={"layer": other, "band": b}, device_id_type=MESH)

    @pl.when(layer == 0)
    def _():
        pl.semaphore_wait(x_ready, 1)

    def to_x(src, dst, send, recv):
        return pltpu.make_async_remote_copy(
            src_ref=src, dst_ref=dst, send_sem=send, recv_sem=recv,
            device_id={"layer": other, "band": b}, device_id_type=MESH)

    def to_band(src, dst, send, recv, peer):
        return pltpu.make_async_remote_copy(
            src_ref=src, dst_ref=dst, send_sem=send, recv_sem=recv,
            device_id={"layer": layer, "band": peer}, device_id_type=MESH)

    h_across = [
        to_x(h_hbm.at[b, pl.ds(0, 5)], hx.at[b, pl.ds(0, 5)], hx_send.at[0], hx_recv.at[0]),
        to_x(h_hbm.at[b, pl.ds(own_cross, 1)], hx.at[b, pl.ds(5, 1)], hx_send.at[1], hx_recv.at[1]),
    ]
    n_across = to_x(nbr_hbm, nx_v, n_send.at[0], n_recv.at[0])
    c_across = [
        to_x(c_hbm.at[:, :, pl.ds(place(s, other), n)], cx[s], c_send.at[s], c_recv.at[s]) for s in range(count)
    ]
    for copy in h_across + [n_across] + c_across[:last]:
        copy.start()

    n_copy = pltpu.make_async_copy(nbr_hbm, nown, misc_sem.at[0])
    occ_copy = pltpu.make_async_copy(occ_hbm.at[:, pl.ds(pl.multiple_of(b * nbl, n), nbl)], occ_v, misc_sem.at[2])
    basis_copy = pltpu.make_async_copy(basis_hbm.at[0], functions, misc_sem.at[3])
    h_copies = [
        pltpu.make_async_copy(h_hbm.at[:, pl.ds(0, 5)], hown.at[:, pl.ds(0, 5)], lh_sem.at[0]),
        pltpu.make_async_copy(h_hbm.at[:, pl.ds(own_cross, 1)], hown.at[:, pl.ds(5, 1)], lh_sem.at[1]),
    ]
    c_copies = [
        pltpu.make_async_copy(c_hbm.at[:, :, pl.ds(place(s), n)], cown[s], lc_sem.at[s]) for s in range(count)
    ]
    for copy in [n_copy, occ_copy] + h_copies + c_copies + [basis_copy]:
        copy.start()

    @pl.when(layer == 0)
    def _():
        for peer in [core_peer] + [(site + k) % half * 2 + core for k in range(1, half)]:
            pl.semaphore_signal(barrier, inc=1, device_id={"layer": layer, "band": peer}, device_id_type=MESH)
        pl.semaphore_wait(barrier, half)
        pl.semaphore_signal(all_in, inc=1, device_id={"layer": other, "band": b}, device_id_type=MESH)

    @pl.when(layer == 1)
    def _():
        pl.semaphore_wait(all_in, 1)

    sent = []

    def forward(block, peer):
        slot = len(sent)
        copy = to_band(hx.at[block], hx.at[block], f_send.at[slot], f_recv.at[block], peer)
        copy.start()
        sent.append(copy)

    def arrived(block, peer):
        to_band(hx.at[block], hx.at[block], f_send.at[0], f_recv.at[block], peer).wait_recv()

    y_peer = ident(z, 1 - y, core)
    for copy in h_across:
        copy.wait_recv()
    for k in range(1, nz):
        forward(b, ident((z + k) % nz, y, core))
    forward(b, y_peer)
    forward(b, core_peer)
    for k in range(1, nz):
        block = ident((z - k + nz) % nz, y, core)
        arrived(block, block)
        forward(block, y_peer)
        forward(block, core_peer)
    for k in range(nz):
        block = ident((z - k + nz) % nz, 1 - y, core)
        arrived(block, y_peer)
        forward(block, core_peer)
    for k in range(nz):
        for yy in (y, 1 - y):
            arrived(ident((z - k + nz) % nz, yy, 1 - core), core_peer)

    n_across.wait_recv()
    nx_copy = pltpu.make_async_copy(nx_v, nx, misc_sem.at[1])
    nx_copy.start()
    for copy in [n_copy, nx_copy, occ_copy] + h_copies:
        copy.wait()

    def image(blocks, table, e, cross, near, far):
        row = jnp.concatenate([blocks[e, k] for k in range(6)], axis=1)
        parts = [near[lax.rem(table[k, e], elements)] for k in range(5)]
        parts.append(far[lax.rem(table[cross, e], elements)])
        return jnp.dot(row, jnp.concatenate(parts, axis=0), preferred_element_type=jnp.float32)

    def once(got, start):
        return ((got - center * start.astype(jnp.float32)) * (1.0 / half_width)).astype(jnp.bfloat16)

    def twice(got, middle, start):
        value = (got - center * middle.astype(jnp.float32)) * (2.0 / half_width) - start.astype(jnp.float32)
        return value.astype(jnp.bfloat16)

    def square(value, weight):
        scaled = (value.astype(jnp.float32) * weight).astype(jnp.bfloat16)
        return lax.dot_general(scaled, value, (((1,), (1,)), ((), ())), preferred_element_type=jnp.float32)

    def pairs(body):
        def both(t, carry):
            body([2 * t, 2 * t + 1])
            return carry
        lax.fori_loop(0, elements // 2, both, 0)

    def filter_chunk(s):
        c_copies[s].wait()
        c_across[s].wait_recv()
        own, far = cown[s], cx[s]
        weight = (1 + occ_v[:, pl.ds(place(s), n)]).astype(jnp.float32)

        def first(at):
            mine = [once(image(hown, nown, e, own_cross, own, far), own[e]) for e in at]
            theirs = [once(image(hx, nx, e, x_cross, far, own), far[e]) for e in at]
            for e, a, c in zip(at, mine, theirs):
                f1o[e] = a
                f1x[e] = c

        def second(at):
            got = [twice(image(hown, nown, e, own_cross, f1o, f1x), f1o[e], own[e]) for e in at]
            if s < last:
                parts = [square(value, weight) for value in got]
                if s > 0:
                    parts = [part + gram[e] for e, part in zip(at, parts)]
                for e, part in zip(at, parts):
                    gram[e] = part
            for e, value in zip(at, got):
                out_ref[e, :, pl.ds(place(s), n)] = value

        def second_x(at):
            got = [twice(image(hx, nx, e, x_cross, f1x, f1o), f1x[e], far[e]) for e in at]
            for e, part in zip(at, [square(value, weight) for value in got]):
                across[e] = part

        pairs(first)
        pairs(second)
        if s == 0:
            pairs(second_x)

    def reduction(source, gsend, gcore, grecv, k_send, k_recv, g_send, g_recv):
        def to_core(t):
            return to_band(gsend.at[2 * t + 1 - core], gcore.at[t], k_send.at[t], k_recv.at[t], core_peer)

        def to_owner(k):
            element = (site + k) % half * 2 + core
            return to_band(gsend.at[element], grecv.at[k], g_send.at[k], g_recv.at[k], element)

        def pair_up(t, carry):
            gsend[2 * t + 1 - core] = source[2 * t + 1 - core].astype(jnp.bfloat16)
            to_core(t).start()
            return carry

        def hand_over(i, carry):
            k = i + 1
            t = (site + k) % half
            to_core(t).wait_recv()
            gsend[2 * t + core] = (source[2 * t + core] + gcore[t].astype(jnp.float32)).astype(jnp.bfloat16)
            to_owner(k).start()
            return carry

        def begin():
            lax.fori_loop(0, half, pair_up, 0)
            lax.fori_loop(0, half - 1, hand_over, 0)

        def end():
            to_core(site).wait_recv()
            total = source[b] + gcore[site].astype(jnp.float32)
            for k in range(1, half):
                to_owner(k).wait_recv()
                total = total + grecv[k].astype(jnp.float32)
            return total

        def drain():
            for t in range(half):
                to_core(t).wait_send()
            for k in range(1, half):
                to_owner(k).wait_send()

        return begin, end, drain

    begin_a, end_a, drain_a = reduction(across, gsend_a, gcore_a, grecv_a, ka_send, ka_recv, ga_send, ga_recv)
    begin_b, end_b, drain_b = reduction(gram, gsend_b, gcore_b, grecv_b, kb_send, kb_recv, gb_send, gb_recv)
    t_across = to_x(total_out, total_in, t_send.at[0], t_recv.at[0])

    filter_chunk(0)
    begin_a()
    for s in range(1, last):
        if s > 1:
            filter_chunk(s)
            continue
        filter_chunk(s)
        total_out[...] = end_a().astype(jnp.bfloat16)
        t_across.start()
        c_across[last].start()
    begin_b()
    total = end_b()
    t_across.wait_recv()
    total = (total + total_in[...].astype(jnp.float32)) * (1.0 / (2.0 * nbl * nb))

    high = total.astype(jnp.bfloat16)
    low = (total - high.astype(jnp.float32)).astype(jnp.bfloat16)
    basis_copy.wait()
    values = functions[...]
    image_g = jnp.dot(values, high, preferred_element_type=jnp.float32)
    image_g = image_g + jnp.dot(values, low, preferred_element_type=jnp.float32)
    product = image_g * values.astype(jnp.float32)
    top = product.astype(jnp.bfloat16)
    rest = (product - top.astype(jnp.float32)).astype(jnp.bfloat16)
    ones = jnp.ones((16, product.shape[1]), jnp.bfloat16)
    over_last = (((1,), (1,)), ((), ()))
    density = lax.dot_general(ones, top, over_last, preferred_element_type=jnp.float32)
    density = density + lax.dot_general(ones, rest, over_last, preferred_element_type=jnp.float32)
    dens_ref[...] = density[0:1]

    filter_chunk(last)

    for copy in h_across + [n_across, t_across] + c_across + sent:
        copy.wait_send()
    drain_a()
    drain_b()


def plane_body(nb, coeffs, hamilton, neighbors, basis, occupation):
    elements, nbasis, nbl = coeffs.shape
    points = basis.shape[1]
    n = 128
    count = nbl // n
    width = neighbors.shape[1]
    half = nb // 2
    dma = pltpu.SemaphoreType.DMA
    hbm = pl.BlockSpec(memory_space=pl.ANY)
    vmem = pl.BlockSpec(memory_space=pltpu.VMEM)
    forwards = (nb // 4 - 1) + 2 + 2 * (nb // 4 - 1) + nb // 4
    bf16, f32 = jnp.bfloat16, jnp.float32
    chunk = pltpu.VMEM((elements, nbasis, n), bf16)
    rounds = [
        pltpu.VMEM((elements, nbasis, nbasis), bf16),
        pltpu.VMEM((half, nbasis, nbasis), bf16),
        pltpu.VMEM((half, nbasis, nbasis), bf16),
    ]
    operands = [coeffs, hamilton, neighbors.T, occupation.reshape(1, -1), basis]
    operands = [pltpu.with_memory_space_constraint(x, pltpu.HBM) for x in operands]
    return pl.pallas_call(
        functools.partial(kernel, nb, n),
        out_shape=(
            jax.ShapeDtypeStruct(coeffs.shape, bf16),
            jax.ShapeDtypeStruct((1, points), f32),
        ),
        in_specs=[hbm] * 5,
        out_specs=(vmem, vmem),
        scratch_shapes=[chunk] * (2 * count) + [
            chunk, chunk,
            pltpu.VMEM((elements, 6, nbasis, nbasis), bf16),
            pltpu.VMEM((elements, 6, nbasis, nbasis), bf16),
            pltpu.VMEM((width, elements), jnp.int32),
            pltpu.SMEM((width, elements), jnp.int32),
            pltpu.SMEM((width, elements), jnp.int32),
            pltpu.VMEM((1, nbl), jnp.int32),
            pltpu.VMEM((points, nbasis), bf16),
            pltpu.VMEM((elements, nbasis, nbasis), f32),
            pltpu.VMEM((elements, nbasis, nbasis), f32),
        ] + rounds + rounds + [
            pltpu.VMEM((nbasis, nbasis), bf16),
            pltpu.VMEM((nbasis, nbasis), bf16),
            dma((count,)), dma((count,)),
            dma((2,)), dma((2,)),
            dma((1,)), dma((1,)),
            dma((forwards,)), dma((nb,)),
        ] + [dma((half,))] * 8 + [
            dma((1,)), dma((1,)),
            dma((count,)), dma((2,)), dma((4,)),
            pltpu.SemaphoreType.REGULAR, pltpu.SemaphoreType.REGULAR,
        ],
        compiler_params=pltpu.CompilerParams(
            collective_id=0, has_side_effects=True, vmem_limit_bytes=40 * 2**20),
    )(*operands)


def solution(mesh):
    layers, nb = mesh.shape["layer"], mesh.shape["band"]

    def body(coeffs, hamilton, neighbors, basis, occupation):
        elements = coeffs.shape[0]
        one_kernel = (
            layers == 2 and elements == FY * FZ and nb == elements
            and nb % 4 == 0 and nb >= 8 and coeffs.shape[2] % 128 == 0 and coeffs.shape[2] >= 512
            and coeffs.shape[1] == 128 and basis.shape[0] == 1
        )
        if one_kernel:
            return plane_body(nb, coeffs, hamilton, neighbors, basis, occupation)
        return general_body(coeffs, hamilton, neighbors, basis, occupation)

    return jax.shard_map(
        body,
        mesh=mesh,
        in_specs=(
            P("layer", None, "band"),
            P("layer", None, None, None),
            P("layer", None),
            P(("layer", "band"), None, None),
            P(),
        ),
        out_specs=(P("layer", None, "band"), P(("layer", "band"), None)),
        check_vma=False,
    )
```

time: 87.6 us -> 83.6 us (0.954)
  Pallas kernels: 86.7 us -> 80.8 us
  local copies, waits for them, and re-layouts: 0 us -> 2.09 us
    pallas_call x2 -> x1, Pallas kernels: 86.7 us -> 80.8 us  [plane_body(): pl.pallas_call(functools.partial(kernel, nb, n), out_shape=(jax.ShapeDtyp...]
    unnamed x0 -> x2, local copies, waits for them, and re-layouts: none -> 2.09 us
where the time goes in v1:
time: 83.6 us; the launch traced here: 83.5 us
  Pallas kernels  80.8 us (97%)
  local copies, waits for them, and re-layouts  2.09 us (2%)
    pallas_call x1, Pallas kernels, plane_body(): pl.pallas_call(functools.partial(kernel, nb, n), out_shape=(jax.ShapeDtyp...  80.8 us
    unnamed x2, local copies, waits for them, and re-layouts  2.09 us

profile of v1, /device:TPU:0, one launch (start us, length us, event | category | flops | bytes accessed | tf_op | source)
XLA Modules:
  0.0 83.5 jit_solution(12867899691550582292)
XLA Ops:
  0.6 80.8 %shard_map.68 = (bf16[16,128,640]{2,1,0:T(8,128)(2,1)S(1)}, f32[1,1728]{1,0:T(1,128)S(1)}) custom-call(bf16[16,128,640]{2,1,0:T(8,128)(2,1)} %c_hbm.1, bf16[16,7,128,128]{3,2,1,0:T(8,128)(2,1)} %h_hbm.1, s32[7,16]{1,0:T(8,128)} %bitcast.3, s32[1,10240]{1,0:T(1,128)} %bitcast.2, bf16[1,1728,128]{2,1,0:T(8,128)(2,1)} %basis_hbm.1), custom_call_target="tpu_custom_call" | custom-call | tf_op jit(solution)/shard_map/pallas_call | solution.py:348
  81.4 1.5 %copy.9 = bf16[16,128,640]{2,1,0:T(8,128)(2,1)} copy(bf16[16,128,640]{2,1,0:T(8,128)(2,1)S(1)} %get-tuple-element.4) | data formatting | bytes 5242880
  82.9 0.6 copy.10

commit v2 on v1

--- a/solution.py
+++ b/solution.py
@@ -64,14 +64,13 @@
 
 
 def kernel(nb, n, c_hbm, h_hbm, nbr_hbm, occ_hbm, basis_hbm, out_ref, dens_ref, *scratch):
-    elements, _, nbl = c_hbm.shape
-    count = nbl // n
-    cown, cx = scratch[:count], scratch[count:2 * count]
-    (f1o, f1x, hown, hx, nx_v, nown, nx, occ_v, functions, gram, across,
+    elements, nbasis, nbl = c_hbm.shape
+    cx, cl = scratch[:3], scratch[3:5]
+    (cown, ahead, f1o, f1x, hown, hx, nx_v, nown, nx, occ_v, functions, gram, across, row_a, row_b, base,
      gsend_a, gcore_a, grecv_a, gsend_b, gcore_b, grecv_b, total_out, total_in,
      c_send, c_recv, hx_send, hx_recv, n_send, n_recv, f_send, f_recv,
      ka_send, ka_recv, ga_send, ga_recv, kb_send, kb_recv, gb_send, gb_recv, t_send, t_recv,
-     lc_sem, lh_sem, misc_sem, x_ready, all_in) = scratch[2 * count:]
+     lc_sem, lh_sem, misc_sem, x_ready, all_in) = scratch[5:]
     layer, b = lax.axis_index("layer"), lax.axis_index("band")
     other = 1 - layer
     nz = nb // 4
@@ -80,13 +79,15 @@
     z, y, core = b // 4, (b // 2) % 2, b % 2
     core_peer = b + 1 - 2 * core
     own_cross, x_cross = 6 - layer, 6 - other
-    last = count - 1
+    part = nbasis // 2
+    widths = (2 * n, n, n, n)
+    starts = (0, 2 * n, 3 * n, 4 * n)
 
     def ident(zz, yy, cc):
         return zz * 4 + yy * 2 + cc
 
     def place(s, side=layer):
-        return pl.multiple_of((s + side * (last - 2 * s)) * n, n)
+        return pl.multiple_of(starts[s] + side * (nbl - widths[s] - 2 * starts[s]), n)
 
     barrier = pltpu.get_barrier_semaphore()
 
@@ -113,15 +114,20 @@
             src_ref=src, dst_ref=dst, send_sem=send, recv_sem=recv,
             device_id={"layer": layer, "band": peer}, device_id_type=MESH)
 
+    pieces = ((0, 3), (3, 3))
     h_across = [
-        to_x(h_hbm.at[b, pl.ds(0, 5)], hx.at[b, pl.ds(0, 5)], hx_send.at[0], hx_recv.at[0]),
-        to_x(h_hbm.at[b, pl.ds(own_cross, 1)], hx.at[b, pl.ds(5, 1)], hx_send.at[1], hx_recv.at[1]),
+        to_x(h_hbm.at[b, pl.ds(0, 3)], hx.at[b, pl.ds(0, 3)], hx_send.at[0], hx_recv.at[0]),
+        to_x(h_hbm.at[b, pl.ds(3, 2)], hx.at[b, pl.ds(3, 2)], hx_send.at[1], hx_recv.at[1]),
+        to_x(h_hbm.at[b, pl.ds(own_cross, 1)], hx.at[b, pl.ds(5, 1)], hx_send.at[2], hx_recv.at[2]),
     ]
     n_across = to_x(nbr_hbm, nx_v, n_send.at[0], n_recv.at[0])
     c_across = [
-        to_x(c_hbm.at[:, :, pl.ds(place(s, other), n)], cx[s], c_send.at[s], c_recv.at[s]) for s in range(count)
+        to_x(c_hbm.at[:, :, pl.ds(place(s, other), widths[s])], cx[s], c_send.at[s], c_recv.at[s]) for s in range(3)
+    ] + [
+        to_x(c_hbm.at[:, pl.ds(i * part, part), pl.ds(place(3, other), n)], cl[i], c_send.at[3 + i], c_recv.at[3 + i])
+        for i in range(2)
     ]
-    for copy in h_across + [n_across] + c_across[:last]:
+    for copy in h_across + [n_across] + c_across[:4]:
         copy.start()
 
     n_copy = pltpu.make_async_copy(nbr_hbm, nown, misc_sem.at[0])
@@ -131,10 +137,8 @@
         pltpu.make_async_copy(h_hbm.at[:, pl.ds(0, 5)], hown.at[:, pl.ds(0, 5)], lh_sem.at[0]),
         pltpu.make_async_copy(h_hbm.at[:, pl.ds(own_cross, 1)], hown.at[:, pl.ds(5, 1)], lh_sem.at[1]),
     ]
-    c_copies = [
-        pltpu.make_async_copy(c_hbm.at[:, :, pl.ds(place(s), n)], cown[s], lc_sem.at[s]) for s in range(count)
-    ]
-    for copy in [n_copy, occ_copy] + h_copies + c_copies + [basis_copy]:
+    c_copy = pltpu.make_async_copy(c_hbm, cown, lc_sem.at[0])
+    for copy in [n_copy, occ_copy, c_copy] + h_copies + [basis_copy]:
         copy.start()
 
     @pl.when(layer == 0)
@@ -148,99 +152,219 @@
     def _():
         pl.semaphore_wait(all_in, 1)
 
-    sent = []
-
-    def forward(block, peer):
-        slot = len(sent)
-        copy = to_band(hx.at[block], hx.at[block], f_send.at[slot], f_recv.at[block], peer)
-        copy.start()
-        sent.append(copy)
-
-    def arrived(block, peer):
-        to_band(hx.at[block], hx.at[block], f_send.at[0], f_recv.at[block], peer).wait_recv()
-
-    y_peer = ident(z, 1 - y, core)
-    for copy in h_across:
-        copy.wait_recv()
-    for k in range(1, nz):
-        forward(b, ident((z + k) % nz, y, core))
-    forward(b, y_peer)
-    forward(b, core_peer)
-    for k in range(1, nz):
-        block = ident((z - k + nz) % nz, y, core)
-        arrived(block, block)
-        forward(block, y_peer)
-        forward(block, core_peer)
-    for k in range(nz):
-        block = ident((z - k + nz) % nz, 1 - y, core)
-        arrived(block, y_peer)
-        forward(block, core_peer)
-    for k in range(nz):
-        for yy in (y, 1 - y):
-            arrived(ident((z - k + nz) % nz, yy, 1 - core), core_peer)
-
-    n_across.wait_recv()
-    nx_copy = pltpu.make_async_copy(nx_v, nx, misc_sem.at[1])
-    nx_copy.start()
-    for copy in [n_copy, nx_copy, occ_copy] + h_copies:
-        copy.wait()
-
-    def image(blocks, table, e, cross, near, far):
-        row = jnp.concatenate([blocks[e, k] for k in range(6)], axis=1)
-        parts = [near[lax.rem(table[k, e], elements)] for k in range(5)]
-        parts.append(far[lax.rem(table[cross, e], elements)])
-        return jnp.dot(row, jnp.concatenate(parts, axis=0), preferred_element_type=jnp.float32)
-
-    def once(got, start):
-        return ((got - center * start.astype(jnp.float32)) * (1.0 / half_width)).astype(jnp.bfloat16)
-
-    def twice(got, middle, start):
-        value = (got - center * middle.astype(jnp.float32)) * (2.0 / half_width) - start.astype(jnp.float32)
-        return value.astype(jnp.bfloat16)
-
-    def square(value, weight):
-        scaled = (value.astype(jnp.float32) * weight).astype(jnp.bfloat16)
-        return lax.dot_general(scaled, value, (((1,), (1,)), ((), ())), preferred_element_type=jnp.float32)
-
     def pairs(body):
         def both(t, carry):
             body([2 * t, 2 * t + 1])
             return carry
         lax.fori_loop(0, elements // 2, both, 0)
 
+    for copy in [n_copy, c_copy] + h_copies:
+        copy.wait()
+
+    def in_plane(at):
+        def one(e):
+            row = jnp.concatenate([hown[e, k] for k in range(5)], axis=1)
+            parts = jnp.concatenate([cown[lax.rem(nown[k, e], elements)] for k in range(5)], axis=0)
+            return jnp.dot(row, parts, preferred_element_type=jnp.float32) - center * cown[e].astype(jnp.float32)
+        for e, value in zip(at, [one(e) for e in at]):
+            ahead[e] = value
+
+    pairs(in_plane)
+
+    sent = []
+
+    def always(body):
+        body()
+
+    def forward(block, i, peer, when=always):
+        slot = len(sent)
+        at, size = pieces[i]
+        held = hx.at[block, pl.ds(at, size)]
+        copy = to_band(held, held, f_send.at[slot], f_recv.at[block * 2 + i], peer)
+        sent.append((when, copy))
+        when(copy.start)
+
+    def arrived(block, i, peer):
+        at, size = pieces[i]
+        held = hx.at[block, pl.ds(at, size)]
+        to_band(held, held, f_send.at[0], f_recv.at[block * 2 + i], peer).wait_recv()
+
+    def inside(zz):
+        return pl.when(jnp.logical_and(zz >= 0, zz < nz))
+
+    def both_inside(za, zb):
+        return pl.when(jnp.logical_and(jnp.minimum(za, zb) >= 0, jnp.maximum(za, zb) < nz))
+
+    y_peer = ident(z, 1 - y, core)
+    for i in range(2):
+        h_across[i].wait_recv()
+        if i == 1:
+            h_across[2].wait_recv()
+        for step in (1, -1):
+            forward(b, i, ident(z + step, y, core), inside(z + step))
+        forward(b, i, y_peer)
+        forward(b, i, core_peer)
+
+    def over_y(away):
+        for i in range(2):
+            for step in (1, -1) if away else (1,):
+                from_z = z - step * away
+                block = ident(from_z, 1 - y, core)
+                if away:
+                    inside(from_z)(functools.partial(arrived, block, i, y_peer))
+                    forward(block, i, core_peer, inside(from_z))
+                else:
+                    arrived(block, i, y_peer)
+                    forward(block, i, core_peer)
+
+    for away in range(1, nz):
+        for i in range(2):
+            for step in (1, -1):
+                from_z = z - step * away
+                block = ident(from_z, y, core)
+                inside(from_z)(functools.partial(arrived, block, i, ident(z - step, y, core)))
+                forward(block, i, ident(z + step, y, core), both_inside(from_z, z + step))
+                forward(block, i, y_peer, inside(from_z))
+                forward(block, i, core_peer, inside(from_z))
+        over_y(away - 1)
+    over_y(nz - 1)
+    for zz in range(nz):
+        for yy in range(2):
+            for i in range(2):
+                arrived(ident(zz, yy, 1 - core), i, core_peer)
+
+    n_across.wait_recv()
+    nx_copy = pltpu.make_async_copy(nx_v, nx, misc_sem.at[1])
+    nx_copy.start()
+    for copy in [nx_copy, occ_copy]:
+        copy.wait()
+
+    def image(blocks, table, e, cross, near, far):
+        row = jnp.concatenate([blocks[e, k] for k in range(6)], axis=1)
+        parts = [near(lax.rem(table[k, e], elements)) for k in range(5)]
+        parts.append(far(lax.rem(table[cross, e], elements)))
+        return jnp.dot(row, jnp.concatenate(parts, axis=0), preferred_element_type=jnp.float32)
+
+    def once(got):
+        return (got * (1.0 / half_width)).astype(jnp.bfloat16)
+
+    def twice(got, middle, start):
+        return (got - center * middle.astype(jnp.float32)) * (2.0 / half_width) - start.astype(jnp.float32)
+
+    def square(value, weight):
+        scaled = (value.astype(jnp.float32) * weight).astype(jnp.bfloat16)
+        return lax.dot_general(scaled, value, (((1,), (1,)), ((), ())), preferred_element_type=jnp.float32)
+
     def filter_chunk(s):
-        c_copies[s].wait()
         c_across[s].wait_recv()
-        own, far = cown[s], cx[s]
-        weight = (1 + occ_v[:, pl.ds(place(s), n)]).astype(jnp.float32)
+        width = widths[s]
+        columns = pl.ds(place(s), width)
+        lanes = pl.ds(0, width)
+        weight = (1 + occ_v[:, columns]).astype(jnp.float32)
+
+        def own(e):
+            return cown[e, :, columns]
+
+        def far(e):
+            return cx[s][e]
+
+        def mine(e):
+            return f1o[e, :, lanes]
+
+        def theirs(e):
+            return f1x[e, :, lanes]
 
         def first(at):
-            mine = [once(image(hown, nown, e, own_cross, own, far), own[e]) for e in at]
-            theirs = [once(image(hx, nx, e, x_cross, far, own), far[e]) for e in at]
-            for e, a, c in zip(at, mine, theirs):
-                f1o[e] = a
-                f1x[e] = c
+            across_x = [jnp.dot(hown[e, 5], far(lax.rem(nown[own_cross, e], elements)), preferred_element_type=jnp.float32)
+                        for e in at]
+            left = [once(ahead[e, :, columns] + got) for e, got in zip(at, across_x)]
+            right = [once(image(hx, nx, e, x_cross, far, own) - center * far(e).astype(jnp.float32)) for e in at]
+            for e, p, q in zip(at, left, right):
+                f1o[e, :, lanes] = p
+                f1x[e, :, lanes] = q
 
         def second(at):
-            got = [twice(image(hown, nown, e, own_cross, f1o, f1x), f1o[e], own[e]) for e in at]
-            if s < last:
-                parts = [square(value, weight) for value in got]
+            got = [twice(image(hown, nown, e, own_cross, mine, theirs), mine(e), own(e)).astype(jnp.bfloat16) for e in at]
+            if s < 2:
+                sums = [square(value, weight) for value in got]
                 if s > 0:
-                    parts = [part + gram[e] for e, part in zip(at, parts)]
-                for e, part in zip(at, parts):
-                    gram[e] = part
+                    sums = [added + gram[e] for e, added in zip(at, sums)]
+                for e, added in zip(at, sums):
+                    gram[e] = added
             for e, value in zip(at, got):
-                out_ref[e, :, pl.ds(place(s), n)] = value
+                out_ref[e, :, columns] = value
 
         def second_x(at):
-            got = [twice(image(hx, nx, e, x_cross, f1x, f1o), f1x[e], far[e]) for e in at]
-            for e, part in zip(at, [square(value, weight) for value in got]):
-                across[e] = part
+            got = [twice(image(hx, nx, e, x_cross, theirs, mine), theirs(e), far(e)).astype(jnp.bfloat16) for e in at]
+            for e, added in zip(at, [square(value, weight) for value in got]):
+                across[e] = added
+
+        pairs(first)
+        if s == 0:
+            pairs(second_x)
+        pairs(second)
+
+    last_columns = pl.ds(place(3), n)
+
+    def compose(at):
+        def one(e, k):
+            there = lax.rem(nown[own_cross, e], elements)
+            beside = lax.rem(nown[k, e], elements)
+            if k == 0:
+                which = 0
+            else:
+                target = lax.rem(nown[own_cross, beside], elements)
+                which = 0
+                for j in range(1, 5):
+                    which = jnp.where(lax.rem(nx[j, there], elements) == target, j, which)
+            row = jnp.concatenate([hown[e, k], hown[e, 5]], axis=1)
+            parts = jnp.concatenate([hown[beside, 5], hx[there, which]], axis=0)
+            got = jnp.dot(row, parts, preferred_element_type=jnp.float32)
+            if k == 0:
+                got = got - (2.0 * center) * hown[e, 5].astype(jnp.float32)
+            return (got * (2.0 / half_width / half_width)).astype(jnp.bfloat16)
+        rows = [[one(e, k) for k in range(5)] for e in at]
+        for e, row in zip(at, rows):
+            row_a[e] = jnp.concatenate([block[:, :part] for block in row], axis=1)
+            row_b[e] = jnp.concatenate([block[:, part:] for block in row], axis=1)
+
+    def own_part():
+        def own(e):
+            return cown[e, :, last_columns]
+
+        def mine(e):
+            return f1o[e, :, pl.ds(0, n)]
+
+        def theirs(e):
+            return f1x[e, :, pl.ds(0, n)]
+
+        def first(at):
+            left = [once(ahead[e, :, last_columns]) for e in at]
+            right = [once(jnp.dot(hx[e, 5], own(lax.rem(nx[x_cross, e], elements)), preferred_element_type=jnp.float32))
+                     for e in at]
+            for e, p, q in zip(at, left, right):
+                f1o[e, :, pl.ds(0, n)] = p
+                f1x[e, :, pl.ds(0, n)] = q
+
+        def second(at):
+            got = [twice(image(hown, nown, e, own_cross, mine, theirs), mine(e), own(e)) for e in at]
+            for e, value in zip(at, got):
+                base[e] = value
 
         pairs(first)
         pairs(second)
-        if s == 0:
-            pairs(second_x)
+
+    def far_part(row, held, e):
+        parts = [held[lax.rem(nown[own_cross, lax.rem(nown[k, e], elements)], elements)] for k in range(5)]
+        return base[e] + jnp.dot(row[e], jnp.concatenate(parts, axis=0), preferred_element_type=jnp.float32)
+
+    def far_first(at):
+        for e, value in zip(at, [far_part(row_a, cl[0], e) for e in at]):
+            base[e] = value
+
+    def far_last(at):
+        for e, value in zip(at, [far_part(row_b, cl[1], e) for e in at]):
+            out_ref[e, :, last_columns] = value.astype(jnp.bfloat16)
 
     def reduction(source, gsend, gcore, grecv, k_send, k_recv, g_send, g_recv):
         def to_core(t):
@@ -289,16 +413,17 @@
 
     filter_chunk(0)
     begin_a()
-    for s in range(1, last):
-        if s > 1:
-            filter_chunk(s)
-            continue
-        filter_chunk(s)
-        total_out[...] = end_a().astype(jnp.bfloat16)
-        t_across.start()
-        c_across[last].start()
+    pairs(compose)
+    own_part()
+    filter_chunk(1)
     begin_b()
+    total_out[...] = end_a().astype(jnp.bfloat16)
+    t_across.start()
+    c_across[4].start()
+    filter_chunk(2)
     total = end_b()
+    c_across[3].wait_recv()
+    pairs(far_first)
     t_across.wait_recv()
     total = (total + total_in[...].astype(jnp.float32)) * (1.0 / (2.0 * nbl * nb))
 
@@ -317,27 +442,43 @@
     density = density + lax.dot_general(ones, rest, over_last, preferred_element_type=jnp.float32)
     dens_ref[...] = density[0:1]
 
-    filter_chunk(last)
-
-    for copy in h_across + [n_across, t_across] + c_across + sent:
+    c_across[4].wait_recv()
+    pairs(far_last)
+
+    for copy in h_across + [n_across, t_across] + c_across:
         copy.wait_send()
+    for when, copy in sent:
+        when(copy.wait_send)
     drain_a()
     drain_b()
+
+
+def finish_kernel(filt_ref, dens_ref, filt_hbm, dens_hbm, sem):
+    copies = [
+        pltpu.make_async_copy(filt_ref, filt_hbm, sem.at[0]),
+        pltpu.make_async_copy(dens_ref, dens_hbm, sem.at[1]),
+    ]
+    for copy in copies:
+        copy.start()
+    for copy in copies:
+        copy.wait()
 
 
 def plane_body(nb, coeffs, hamilton, neighbors, basis, occupation):
     elements, nbasis, nbl = coeffs.shape
     points = basis.shape[1]
-    n = 128
-    count = nbl // n
+    n = nbl // 5
     width = neighbors.shape[1]
     half = nb // 2
     dma = pltpu.SemaphoreType.DMA
     hbm = pl.BlockSpec(memory_space=pl.ANY)
     vmem = pl.BlockSpec(memory_space=pltpu.VMEM)
-    forwards = (nb // 4 - 1) + 2 + 2 * (nb // 4 - 1) + nb // 4
+    nz = nb // 4
+    forwards = 2 * (4 + 6 * (nz - 1) + 1 + 2 * (nz - 1))
     bf16, f32 = jnp.bfloat16, jnp.float32
-    chunk = pltpu.VMEM((elements, nbasis, n), bf16)
+    def chunk(rows, columns, dtype=bf16):
+        return pltpu.VMEM((elements, rows, columns), dtype)
+
     rounds = [
         pltpu.VMEM((elements, nbasis, nbasis), bf16),
         pltpu.VMEM((half, nbasis, nbasis), bf16),
@@ -345,7 +486,7 @@
     ]
     operands = [coeffs, hamilton, neighbors.T, occupation.reshape(1, -1), basis]
     operands = [pltpu.with_memory_space_constraint(x, pltpu.HBM) for x in operands]
-    return pl.pallas_call(
+    filtered, density = pl.pallas_call(
         functools.partial(kernel, nb, n),
         out_shape=(
             jax.ShapeDtypeStruct(coeffs.shape, bf16),
@@ -353,8 +494,11 @@
         ),
         in_specs=[hbm] * 5,
         out_specs=(vmem, vmem),
-        scratch_shapes=[chunk] * (2 * count) + [
-            chunk, chunk,
+        scratch_shapes=[
+            chunk(nbasis, 2 * n), chunk(nbasis, n), chunk(nbasis, n),
+            chunk(nbasis // 2, n), chunk(nbasis // 2, n),
+            chunk(nbasis, nbl), chunk(nbasis, nbl, f32),
+            chunk(nbasis, 2 * n), chunk(nbasis, 2 * n),
             pltpu.VMEM((elements, 6, nbasis, nbasis), bf16),
             pltpu.VMEM((elements, 6, nbasis, nbasis), bf16),
             pltpu.VMEM((width, elements), jnp.int32),
@@ -362,23 +506,35 @@
             pltpu.SMEM((width, elements), jnp.int32),
             pltpu.VMEM((1, nbl), jnp.int32),
             pltpu.VMEM((points, nbasis), bf16),
-            pltpu.VMEM((elements, nbasis, nbasis), f32),
-            pltpu.VMEM((elements, nbasis, nbasis), f32),
+            chunk(nbasis, nbasis, f32), chunk(nbasis, nbasis, f32),
+            chunk(nbasis, 5 * nbasis // 2), chunk(nbasis, 5 * nbasis // 2),
+            chunk(nbasis, n, f32),
         ] + rounds + rounds + [
             pltpu.VMEM((nbasis, nbasis), bf16),
             pltpu.VMEM((nbasis, nbasis), bf16),
-            dma((count,)), dma((count,)),
-            dma((2,)), dma((2,)),
+            dma((5,)), dma((5,)),
+            dma((3,)), dma((3,)),
             dma((1,)), dma((1,)),
-            dma((forwards,)), dma((nb,)),
+            dma((forwards,)), dma((2 * nb,)),
         ] + [dma((half,))] * 8 + [
             dma((1,)), dma((1,)),
-            dma((count,)), dma((2,)), dma((4,)),
+            dma((1,)), dma((2,)), dma((4,)),
             pltpu.SemaphoreType.REGULAR, pltpu.SemaphoreType.REGULAR,
         ],
         compiler_params=pltpu.CompilerParams(
-            collective_id=0, has_side_effects=True, vmem_limit_bytes=40 * 2**20),
+            collective_id=0, has_side_effects=True, vmem_limit_bytes=44 * 2**20),
     )(*operands)
+    return pl.pallas_call(
+        finish_kernel,
+        out_shape=(
+            jax.ShapeDtypeStruct(coeffs.shape, bf16),
+            jax.ShapeDtypeStruct((1, points), f32),
+        ),
+        in_specs=[vmem, vmem],
+        out_specs=(hbm, hbm),
+        scratch_shapes=[dma((2,))],
+        compiler_params=pltpu.CompilerParams(vmem_limit_bytes=8 * 2**20),
+    )(filtered, density)
 
 
 def solution(mesh):
@@ -388,7 +544,7 @@
         elements = coeffs.shape[0]
         one_kernel = (
             layers == 2 and elements == FY * FZ and nb == elements
-            and nb % 4 == 0 and nb >= 8 and coeffs.shape[2] % 128 == 0 and coeffs.shape[2] >= 512
+            and nb % 4 == 0 and nb >= 8 and coeffs.shape[2] % 640 == 0
             and coeffs.shape[1] == 128 and basis.shape[0] == 1
         )
         if one_kernel:

time: 83.6 us -> 73.3 us (0.88)
  Pallas kernels: 80.8 us -> 72.5 us
  local copies, waits for them, and re-layouts: 2.09 us -> 0 us
    pallas_call x1, Pallas kernels: 80.8 us -> 71 us  [plane_body(): pl.pallas_call(functools.partial(kernel, nb, n), out_shape=(jax.ShapeDtyp...]
    unnamed x2 -> x0, local copies, waits for them, and re-layouts: 2.09 us -> none
    pallas_call x0 -> x1, Pallas kernels: none -> 1.51 us  [plane_body(): pl.pallas_call(finish_kernel, out_shape=(jax.ShapeDtypeStruct(coeffs.shap...]
where the time goes in v2:
time: 73.3 us; the launch traced here: 73.1 us
  Pallas kernels  72.5 us (99%)
    pallas_call x1, Pallas kernels, plane_body(): pl.pallas_call(functools.partial(kernel, nb, n), out_shape=(jax.ShapeDtyp...  71 us
    pallas_call x1, Pallas kernels, plane_body(): pl.pallas_call(finish_kernel, out_shape=(jax.ShapeDtypeStruct(coeffs.shap...  1.51 us

profile of v2, /device:TPU:0, one launch (start us, length us, event | category | flops | bytes accessed | tf_op | source)
XLA Modules:
  0.0 73.1 jit_solution(13026216164217067615)
XLA Ops:
  0.6 71.0 %shard_map.68 = (bf16[16,128,640]{2,1,0:T(8,128)(2,1)S(1)}, f32[1,1728]{1,0:T(1,128)S(1)}) custom-call(bf16[16,128,640]{2,1,0:T(8,128)(2,1)} %c_hbm.1, bf16[16,7,128,128]{3,2,1,0:T(8,128)(2,1)} %h_hbm.1, s32[7,16]{1,0:T(8,128)} %bitcast.3, s32[1,10240]{1,0:T(1,128)} %bitcast.2, bf16[1,1728,128]{2,1,0:T(8,128)(2,1)} %basis_hbm.1), custom_call_target="tpu_custom_call" | custom-call | tf_op jit(solution)/shard_map/pallas_call | solution.py:489
  71.6 1.5 %shard_map.69 = (bf16[16,128,640]{2,1,0:T(8,128)(2,1)}, f32[1,1728]{1,0:T(1,128)}) custom-call(bf16[16,128,640]{2,1,0:T(8,128)(2,1)S(1)} %get-tuple-element.4.filt_ref, f32[1,1728]{1,0:T(1,128)S(1)} %get-tuple-element.5.dens_ref), custom_call_target="tpu_custom_call" | custom-call | tf_op jit(solution)/shard_map/pallas_call | solution.py:527

commit v3 on v2

--- a/solution.py
+++ b/solution.py
@@ -79,7 +79,8 @@
     z, y, core = b // 4, (b // 2) % 2, b % 2
     core_peer = b + 1 - 2 * core
     own_cross, x_cross = 6 - layer, 6 - other
-    part = nbasis // 2
+    part = nbasis - nbasis // 2
+    row_parts = (pl.ds(0, part), pl.ds(part, nbasis - part))
     widths = (2 * n, n, n, n)
     starts = (0, 2 * n, 3 * n, 4 * n)
 
@@ -124,7 +125,7 @@
     c_across = [
         to_x(c_hbm.at[:, :, pl.ds(place(s, other), widths[s])], cx[s], c_send.at[s], c_recv.at[s]) for s in range(3)
     ] + [
-        to_x(c_hbm.at[:, pl.ds(i * part, part), pl.ds(place(3, other), n)], cl[i], c_send.at[3 + i], c_recv.at[3 + i])
+        to_x(c_hbm.at[:, row_parts[i], pl.ds(place(3, other), n)], cl[i], c_send.at[3 + i], c_recv.at[3 + i])
         for i in range(2)
     ]
     for copy in h_across + [n_across] + c_across[:4]:
@@ -152,11 +153,14 @@
     def _():
         pl.semaphore_wait(all_in, 1)
 
+    def groups(body, size, low=0, high=elements):
+        def several(t, carry):
+            body([size * t + i for i in range(size)])
+            return carry
+        lax.fori_loop(low // size, high // size, several, 0)
+
     def pairs(body):
-        def both(t, carry):
-            body([2 * t, 2 * t + 1])
-            return carry
-        lax.fori_loop(0, elements // 2, both, 0)
+        groups(body, 2)
 
     for copy in [n_copy, c_copy] + h_copies:
         copy.wait()
@@ -169,8 +173,6 @@
         for e, value in zip(at, [one(e) for e in at]):
             ahead[e] = value
 
-    pairs(in_plane)
-
     sent = []
 
     def always(body):
@@ -196,6 +198,7 @@
         return pl.when(jnp.logical_and(jnp.minimum(za, zb) >= 0, jnp.maximum(za, zb) < nz))
 
     y_peer = ident(z, 1 - y, core)
+    groups(in_plane, 2, 0, 8)
     for i in range(2):
         h_across[i].wait_recv()
         if i == 1:
@@ -204,6 +207,7 @@
             forward(b, i, ident(z + step, y, core), inside(z + step))
         forward(b, i, y_peer)
         forward(b, i, core_peer)
+    groups(in_plane, 2, 8, elements)
 
     def over_y(away):
         for i in range(2):
@@ -299,10 +303,11 @@
             for e, added in zip(at, [square(value, weight) for value in got]):
                 across[e] = added
 
-        pairs(first)
+        size = 4
+        groups(first, size)
         if s == 0:
-            pairs(second_x)
-        pairs(second)
+            groups(second_x, size)
+        groups(second, size)
 
     last_columns = pl.ds(place(3), n)
 
@@ -351,8 +356,8 @@
             for e, value in zip(at, got):
                 base[e] = value
 
-        pairs(first)
-        pairs(second)
+        groups(first, 4)
+        groups(second, 4)
 
     def far_part(row, held, e):
         parts = [held[lax.rem(nown[own_cross, lax.rem(nown[k, e], elements)], elements)] for k in range(5)]
@@ -389,6 +394,8 @@
 
         def begin():
             lax.fori_loop(0, half, pair_up, 0)
+
+        def pass_on():
             lax.fori_loop(0, half - 1, hand_over, 0)
 
         def end():
@@ -405,25 +412,27 @@
             for k in range(1, half):
                 to_owner(k).wait_send()
 
-        return begin, end, drain
-
-    begin_a, end_a, drain_a = reduction(across, gsend_a, gcore_a, grecv_a, ka_send, ka_recv, ga_send, ga_recv)
-    begin_b, end_b, drain_b = reduction(gram, gsend_b, gcore_b, grecv_b, kb_send, kb_recv, gb_send, gb_recv)
+        return begin, pass_on, end, drain
+
+    begin_a, pass_a, end_a, drain_a = reduction(across, gsend_a, gcore_a, grecv_a, ka_send, ka_recv, ga_send, ga_recv)
+    begin_b, pass_b, end_b, drain_b = reduction(gram, gsend_b, gcore_b, grecv_b, kb_send, kb_recv, gb_send, gb_recv)
     t_across = to_x(total_out, total_in, t_send.at[0], t_recv.at[0])
 
     filter_chunk(0)
     begin_a()
     pairs(compose)
+    pass_a()
     own_part()
     filter_chunk(1)
     begin_b()
     total_out[...] = end_a().astype(jnp.bfloat16)
     t_across.start()
     c_across[4].start()
+    pass_b()
     filter_chunk(2)
     total = end_b()
     c_across[3].wait_recv()
-    pairs(far_first)
+    groups(far_first, 4)
     t_across.wait_recv()
     total = (total + total_in[...].astype(jnp.float32)) * (1.0 / (2.0 * nbl * nb))
 
@@ -443,7 +452,7 @@
     dens_ref[...] = density[0:1]
 
     c_across[4].wait_recv()
-    pairs(far_last)
+    groups(far_last, 4)
 
     for copy in h_across + [n_across, t_across] + c_across:
         copy.wait_send()
@@ -496,7 +505,7 @@
         out_specs=(vmem, vmem),
         scratch_shapes=[
             chunk(nbasis, 2 * n), chunk(nbasis, n), chunk(nbasis, n),
-            chunk(nbasis // 2, n), chunk(nbasis // 2, n),
+            chunk(nbasis - nbasis // 2, n), chunk(nbasis // 2, n),
             chunk(nbasis, nbl), chunk(nbasis, nbl, f32),
             chunk(nbasis, 2 * n), chunk(nbasis, 2 * n),
             pltpu.VMEM((elements, 6, nbasis, nbasis), bf16),
@@ -507,7 +516,7 @@
             pltpu.VMEM((1, nbl), jnp.int32),
             pltpu.VMEM((points, nbasis), bf16),
             chunk(nbasis, nbasis, f32), chunk(nbasis, nbasis, f32),
-            chunk(nbasis, 5 * nbasis // 2), chunk(nbasis, 5 * nbasis // 2),
+            chunk(nbasis, 5 * (nbasis - nbasis // 2)), chunk(nbasis, 5 * (nbasis // 2)),
             chunk(nbasis, n, f32),
         ] + rounds + rounds + [
             pltpu.VMEM((nbasis, nbasis), bf16),

time: 73.3 us -> 70.3 us (0.959)
  Pallas kernels: 72.5 us -> 69.5 us
    pallas_call x1, Pallas kernels: 71 us -> 68 us  [plane_body(): pl.pallas_call(functools.partial(kernel, nb, n), out_shape=(jax.ShapeDtyp...]
where the time goes in v3:
time: 70.3 us; the launch traced here: 70.2 us
  Pallas kernels  69.5 us (99%)
    pallas_call x1, Pallas kernels, plane_body(): pl.pallas_call(functools.partial(kernel, nb, n), out_shape=(jax.ShapeDtyp...  68 us
    pallas_call x1, Pallas kernels, plane_body(): pl.pallas_call(finish_kernel, out_shape=(jax.ShapeDtypeStruct(coeffs.shap...  1.51 us

profile of v3, /device:TPU:0, one launch (start us, length us, event | category | flops | bytes accessed | tf_op | source)
XLA Modules:
  0.0 70.2 jit_solution(7377252639776442287)
XLA Ops:
  0.6 68.0 %shard_map.68 = (bf16[16,128,640]{2,1,0:T(8,128)(2,1)S(1)}, f32[1,1728]{1,0:T(1,128)S(1)}) custom-call(bf16[16,128,640]{2,1,0:T(8,128)(2,1)} %c_hbm.1, bf16[16,7,128,128]{3,2,1,0:T(8,128)(2,1)} %h_hbm.1, s32[7,16]{1,0:T(8,128)} %bitcast.3, s32[1,10240]{1,0:T(1,128)} %bitcast.2, bf16[1,1728,128]{2,1,0:T(8,128)(2,1)} %basis_hbm.1), custom_call_target="tpu_custom_call" | custom-call | tf_op jit(solution)/shard_map/pallas_call | solution.py:498
  68.7 1.5 %shard_map.69 = (bf16[16,128,640]{2,1,0:T(8,128)(2,1)}, f32[1,1728]{1,0:T(1,128)}) custom-call(bf16[16,128,640]{2,1,0:T(8,128)(2,1)S(1)} %get-tuple-element.4.filt_ref, f32[1,1728]{1,0:T(1,128)S(1)} %get-tuple-element.5.dens_ref), custom_call_target="tpu_custom_call" | custom-call | tf_op jit(solution)/shard_map/pallas_call | solution.py:536

commit v4 on v3

--- a/solution.py
+++ b/solution.py
@@ -79,7 +79,7 @@
     z, y, core = b // 4, (b // 2) % 2, b % 2
     core_peer = b + 1 - 2 * core
     own_cross, x_cross = 6 - layer, 6 - other
-    part = nbasis - nbasis // 2
+    part = nbasis - nbasis // 4
     row_parts = (pl.ds(0, part), pl.ds(part, nbasis - part))
     widths = (2 * n, n, n, n)
     starts = (0, 2 * n, 3 * n, 4 * n)
@@ -128,7 +128,7 @@
         to_x(c_hbm.at[:, row_parts[i], pl.ds(place(3, other), n)], cl[i], c_send.at[3 + i], c_recv.at[3 + i])
         for i in range(2)
     ]
-    for copy in h_across + [n_across] + c_across[:4]:
+    for copy in h_across + [n_across] + c_across[:3]:
         copy.start()
 
     n_copy = pltpu.make_async_copy(nbr_hbm, nown, misc_sem.at[0])
@@ -423,16 +423,15 @@
     pairs(compose)
     pass_a()
     own_part()
+    total_out[...] = end_a().astype(jnp.bfloat16)
+    t_across.start()
+    for copy in c_across[3:]:
+        copy.start()
     filter_chunk(1)
     begin_b()
-    total_out[...] = end_a().astype(jnp.bfloat16)
-    t_across.start()
-    c_across[4].start()
     pass_b()
     filter_chunk(2)
     total = end_b()
-    c_across[3].wait_recv()
-    groups(far_first, 4)
     t_across.wait_recv()
     total = (total + total_in[...].astype(jnp.float32)) * (1.0 / (2.0 * nbl * nb))
 
@@ -451,15 +450,18 @@
     density = density + lax.dot_general(ones, rest, over_last, preferred_element_type=jnp.float32)
     dens_ref[...] = density[0:1]
 
-    c_across[4].wait_recv()
-    groups(far_last, 4)
-
-    for copy in h_across + [n_across, t_across] + c_across:
+    c_across[3].wait_recv()
+    groups(far_first, 16)
+
+    for copy in h_across + [n_across, t_across] + c_across[:4]:
         copy.wait_send()
     for when, copy in sent:
         when(copy.wait_send)
     drain_a()
     drain_b()
+    c_across[4].wait_recv()
+    groups(far_last, 16)
+    c_across[4].wait_send()
 
 
 def finish_kernel(filt_ref, dens_ref, filt_hbm, dens_hbm, sem):
@@ -505,7 +507,7 @@
         out_specs=(vmem, vmem),
         scratch_shapes=[
             chunk(nbasis, 2 * n), chunk(nbasis, n), chunk(nbasis, n),
-            chunk(nbasis - nbasis // 2, n), chunk(nbasis // 2, n),
+            chunk(nbasis - nbasis // 4, n), chunk(nbasis // 4, n),
             chunk(nbasis, nbl), chunk(nbasis, nbl, f32),
             chunk(nbasis, 2 * n), chunk(nbasis, 2 * n),
             pltpu.VMEM((elements, 6, nbasis, nbasis), bf16),
@@ -516,7 +518,7 @@
             pltpu.VMEM((1, nbl), jnp.int32),
             pltpu.VMEM((points, nbasis), bf16),
             chunk(nbasis, nbasis, f32), chunk(nbasis, nbasis, f32),
-            chunk(nbasis, 5 * (nbasis - nbasis // 2)), chunk(nbasis, 5 * (nbasis // 2)),
+            chunk(nbasis, 5 * (nbasis - nbasis // 4)), chunk(nbasis, 5 * (nbasis // 4)),
             chunk(nbasis, n, f32),
         ] + rounds + rounds + [
             pltpu.VMEM((nbasis, nbasis), bf16),

time: 70.3 us -> 69.6 us (0.990)
  no operation moved by 1% of the time
where the time goes in v4:
time: 69.6 us; the launch traced here: 69.5 us
  Pallas kernels  68.8 us (99%)
    pallas_call x1, Pallas kernels, plane_body(): pl.pallas_call(functools.partial(kernel, nb, n), out_shape=(jax.ShapeDtyp...  67.3 us
    pallas_call x1, Pallas kernels, plane_body(): pl.pallas_call(finish_kernel, out_shape=(jax.ShapeDtypeStruct(coeffs.shap...  1.51 us

profile of v4, /device:TPU:0, one launch (start us, length us, event | category | flops | bytes accessed | tf_op | source)
XLA Modules:
  0.0 69.5 jit_solution(1039046010302851551)
XLA Ops:
  0.6 67.3 %shard_map.68 = (bf16[16,128,640]{2,1,0:T(8,128)(2,1)S(1)}, f32[1,1728]{1,0:T(1,128)S(1)}) custom-call(bf16[16,128,640]{2,1,0:T(8,128)(2,1)} %c_hbm.1, bf16[16,7,128,128]{3,2,1,0:T(8,128)(2,1)} %h_hbm.1, s32[7,16]{1,0:T(8,128)} %bitcast.3, s32[1,10240]{1,0:T(1,128)} %bitcast.2, bf16[1,1728,128]{2,1,0:T(8,128)(2,1)} %basis_hbm.1), custom_call_target="tpu_custom_call" | custom-call | tf_op jit(solution)/shard_map/pallas_call | solution.py:500
  68.0 1.5 %shard_map.69 = (bf16[16,128,640]{2,1,0:T(8,128)(2,1)}, f32[1,1728]{1,0:T(1,128)}) custom-call(bf16[16,128,640]{2,1,0:T(8,128)(2,1)S(1)} %get-tuple-element.4.filt_ref, f32[1,1728]{1,0:T(1,128)S(1)} %get-tuple-element.5.dens_ref), custom_call_target="tpu_custom_call" | custom-call | tf_op jit(solution)/shard_map/pallas_call | solution.py:538

commit v5 on v4

--- a/solution.py
+++ b/solution.py
@@ -70,7 +70,7 @@
      gsend_a, gcore_a, grecv_a, gsend_b, gcore_b, grecv_b, total_out, total_in,
      c_send, c_recv, hx_send, hx_recv, n_send, n_recv, f_send, f_recv,
      ka_send, ka_recv, ga_send, ga_recv, kb_send, kb_recv, gb_send, gb_recv, t_send, t_recv,
-     lc_sem, lh_sem, misc_sem, x_ready, all_in) = scratch[5:]
+     lc_sem, lh_sem, misc_sem, x_ready, all_in, hold, d_send, d_recv) = scratch[5:]
     layer, b = lax.axis_index("layer"), lax.axis_index("band")
     other = 1 - layer
     nz = nb // 4
@@ -128,7 +128,16 @@
         to_x(c_hbm.at[:, row_parts[i], pl.ds(place(3, other), n)], cl[i], c_send.at[3 + i], c_recv.at[3 + i])
         for i in range(2)
     ]
-    for copy in h_across + [n_across] + c_across[:3]:
+    eased = b < 2
+    helps = jnp.logical_or(b == 2, b == 5)
+    helped = jnp.maximum(b - 2, 0) // 3
+    detour = to_x(h_hbm.at[helped, pl.ds(own_cross, 1)], hold, d_send.at[0], d_recv.at[0])
+    relay = to_band(hold, hx.at[helped, pl.ds(5, 1)], d_send.at[1], hx_recv.at[2], helped)
+    h_across[0].start()
+    h_across[1].start()
+    pl.when(jnp.logical_not(eased))(h_across[2].start)
+    pl.when(helps)(detour.start)
+    for copy in [n_across] + c_across[:3]:
         copy.start()
 
     n_copy = pltpu.make_async_copy(nbr_hbm, nown, misc_sem.at[0])
@@ -207,6 +216,12 @@
             forward(b, i, ident(z + step, y, core), inside(z + step))
         forward(b, i, y_peer)
         forward(b, i, core_peer)
+
+    @pl.when(helps)
+    def _():
+        detour.wait_recv()
+        relay.start()
+
     groups(in_plane, 2, 8, elements)
 
     def over_y(away):
@@ -453,7 +468,10 @@
     c_across[3].wait_recv()
     groups(far_first, 16)
 
-    for copy in h_across + [n_across, t_across] + c_across[:4]:
+    pl.when(jnp.logical_not(eased))(h_across[2].wait_send)
+    pl.when(helps)(detour.wait_send)
+    pl.when(helps)(relay.wait_send)
+    for copy in [h_across[0], h_across[1], n_across, t_across] + c_across[:4]:
         copy.wait_send()
     for when, copy in sent:
         when(copy.wait_send)
@@ -531,6 +549,7 @@
             dma((1,)), dma((1,)),
             dma((1,)), dma((2,)), dma((4,)),
             pltpu.SemaphoreType.REGULAR, pltpu.SemaphoreType.REGULAR,
+            pltpu.VMEM((1, nbasis, nbasis), bf16), dma((2,)), dma((1,)),
         ],
         compiler_params=pltpu.CompilerParams(
             collective_id=0, has_side_effects=True, vmem_limit_bytes=44 * 2**20),

time: 69.6 us -> 69 us (level)
  no operation moved by 1% of the time
where the time goes in v5:
time: 69 us; the launch traced here: 68.8 us
  Pallas kernels  68.2 us (99%)
    pallas_call x1, Pallas kernels, plane_body(): pl.pallas_call(functools.partial(kernel, nb, n), out_shape=(jax.ShapeDtyp...  66.7 us
    pallas_call x1, Pallas kernels, plane_body(): pl.pallas_call(finish_kernel, out_shape=(jax.ShapeDtypeStruct(coeffs.shap...  1.51 us

profile of v5, /device:TPU:0, one launch (start us, length us, event | category | flops | bytes accessed | tf_op | source)
XLA Modules:
  0.0 68.8 jit_solution(866261340768598521)
XLA Ops:
  0.6 66.7 %shard_map.68 = (bf16[16,128,640]{2,1,0:T(8,128)(2,1)S(1)}, f32[1,1728]{1,0:T(1,128)S(1)}) custom-call(bf16[16,128,640]{2,1,0:T(8,128)(2,1)} %c_hbm.1, bf16[16,7,128,128]{3,2,1,0:T(8,128)(2,1)} %h_hbm.1, s32[7,16]{1,0:T(8,128)} %bitcast.3, s32[1,10240]{1,0:T(1,128)} %bitcast.2, bf16[1,1728,128]{2,1,0:T(8,128)(2,1)} %basis_hbm.1), custom_call_target="tpu_custom_call" | custom-call | tf_op jit(solution)/shard_map/pallas_call | solution.py:518
  67.3 1.5 %shard_map.69 = (bf16[16,128,640]{2,1,0:T(8,128)(2,1)}, f32[1,1728]{1,0:T(1,128)}) custom-call(bf16[16,128,640]{2,1,0:T(8,128)(2,1)S(1)} %get-tuple-element.4.filt_ref, f32[1,1728]{1,0:T(1,128)S(1)} %get-tuple-element.5.dens_ref), custom_call_target="tpu_custom_call" | custom-call | tf_op jit(solution)/shard_map/pallas_call | solution.py:557
